TPU v7x, 32 devices: a whole 2x2x4 slice. The times are simulated.
32 devices in a mesh: groups: 2 (over y), uv: 4 (over z), pol: 2 (over x), sub: 2 (over core).
Axes of the slice: x: 2, y: 2, z: 4, core: 2. Of those that a mesh axis runs over, the one named last changes fastest.
Arguments:
- visibilities: bfloat16 [2, 512, 256, 512], P(None, 'uv', 'groups', ('pol', 'sub')), parts along dimension 2, may hold values from -6 to 6
- flags: int32 [1024], P(('groups', 'uv')), parts along dimension 0, may hold values 0 or 1
- delays: int32 [512, 512], replicated, may hold values from 0 to 1023, as said below
- coord_u: int32 [512], replicated, may hold values from 0 to 127
- coord_v: int32 [512], replicated, may hold values from 0 to 63
Outputs:
- images: float32 [1024, 128, 128], P(('groups', 'uv', 'pol', 'sub')), parts along dimension 0
- snr: float32 [1024], P(('groups', 'uv', 'pol', 'sub')), parts along dimension 0
There are 2 independent parts, one for each index of `groups`. A program takes and returns all parts, laid end to end along the dimension named above; an argument that names none is the same for every part. Nothing has to cross between parts.
Inputs may be any that keep to these rules, and one draw needn't show every extreme that they name: delays grow with the DM trial and fall with the channel index, with a small irregular part and a common offset, taken modulo 8 * 128.
All inputs are finite; a program needn't handle non-finite values. No bound on the sum of `flags` on one device may be relied on, other than what follows from the above.
Results may differ from a plain program's by a relative error of at most 0.0003.
Values sent between devices are 32-bit elements; how exact they have to be, the bound alone decides.
No kernel may reach another device: no remote copies, remote signals or barrier semaphores. Data moves between devices by JAX's collectives and lax.ppermute only.
A program may use at most 64 MiB of HBM per device.

v0:
```python
import math

import jax
import jax.numpy as jnp
from jax import lax
from jax.sharding import PartitionSpec as P

IMG = 128
FRAC = 8


def twiddle(length):
    steps = jnp.arange(length, dtype=jnp.int32)
    angle = (steps[:, None] * steps[None, :] % length).astype(jnp.float32) * (
        2.0 * math.pi / length
    )
    return (jnp.cos(angle), jnp.sin(angle))


def spectrum(samples):
    cosine, sine = twiddle(samples.shape[2])
    precise = lax.Precision.HIGHEST
    spectrum_real = jnp.einsum("ft,ctk->cfk", cosine, samples[0], precision=precise) + jnp.einsum(
        "ft,ctk->cfk", sine, samples[1], precision=precise
    )
    spectrum_imag = jnp.einsum("ft,ctk->cfk", cosine, samples[1], precision=precise) - jnp.einsum(
        "ft,ctk->cfk", sine, samples[0], precision=precise
    )
    return (spectrum_real, spectrum_imag)


def signed_frequencies(length):
    steps = jnp.arange(length, dtype=jnp.int32)
    return jnp.where(steps >= length // 2, steps - length, steps)


def rotation(delay_rows, frequencies, cycle):
    index = delay_rows[:, :, None] * frequencies[None, None, :] % cycle
    angle = index.astype(jnp.float32) * (2.0 * math.pi / cycle)
    angle = angle.reshape(delay_rows.shape[0], delay_rows.shape[1] * frequencies.shape[0])
    return (jnp.cos(angle), jnp.sin(angle))


def picture(sum_real, sum_imag, coord_u, coord_v, side, weight):
    precise = lax.Precision.HIGHEST
    pixels = jnp.arange(side, dtype=jnp.int32)
    row_angle = (pixels[:, None] * coord_u[None, :] % side).astype(jnp.float32) * (
        2.0 * math.pi / side
    )
    column_angle = (coord_v[:, None] * pixels[None, :] % side).astype(jnp.float32) * (
        2.0 * math.pi / side
    )
    row_cosine, row_sine = (jnp.cos(row_angle), jnp.sin(row_angle))
    first = sum_real[:, None, :] * row_cosine[None] - sum_imag[:, None, :] * row_sine[None]
    second = sum_real[:, None, :] * row_sine[None] + sum_imag[:, None, :] * row_cosine[None]
    image = jnp.einsum("dlk,km->dlm", first, jnp.cos(column_angle), precision=precise) - jnp.einsum(
        "dlk,km->dlm", second, jnp.sin(column_angle), precision=precise
    )
    return image * weight


def dedisperse(table_rows, frequencies, right_real, right_imag, cycle, scale):
    precise = lax.Precision.HIGHEST
    cosine, sine = rotation(table_rows, frequencies, cycle)
    sum_real = jnp.dot(cosine, right_real, precision=precise) - jnp.dot(
        sine, right_imag, precision=precise
    )
    sum_imag = jnp.dot(sine, right_real, precision=precise) + jnp.dot(
        cosine, right_imag, precision=precise
    )
    return (sum_real * scale, sum_imag * scale)


def shards(visibilities, flags, delays, coord_u, coord_v):
    samples = visibilities.astype(jnp.float32)
    channels = samples.shape[1]
    times = samples.shape[2]
    cells = samples.shape[3]
    total_channels = delays.shape[1]
    spectrum_real, spectrum_imag = spectrum(samples)
    keep = flags.astype(jnp.float32)[:, None, None]
    spectrum_real = spectrum_real * keep
    spectrum_imag = spectrum_imag * keep
    position = lax.axis_index("uv")
    frequencies = signed_frequencies(times)
    cycle = FRAC * times
    scale = 1.0 / math.sqrt(total_channels * times)
    table_rows = lax.dynamic_slice_in_dim(delays, position * channels, channels, 1)
    right_real = spectrum_real.reshape(channels * times, cells)
    right_imag = spectrum_imag.reshape(channels * times, cells)
    part_real, part_imag = dedisperse(table_rows, frequencies, right_real, right_imag, cycle, scale)
    dedispersed = lax.psum_scatter(
        jnp.concatenate([part_real, part_imag], axis=1), "uv", scatter_dimension=0, tiled=True
    )
    halves = dedispersed.reshape(dedispersed.shape[0], 2, cells)
    weight = 2.0 / math.sqrt(coord_u.shape[0])
    planes = lax.all_to_all(halves, ("pol", "sub"), split_axis=0, concat_axis=2, tiled=True)
    images = picture(planes[:, 0], planes[:, 1], coord_u, coord_v, IMG, weight)
    peaks = jnp.max(images, axis=(1, 2))
    power = jnp.mean(images * images, axis=(1, 2))
    snr = peaks / jnp.sqrt(power + 1e-06)
    return (images, snr)


def solution(mesh):
    in_specs = (P(None, "uv", "groups", ("pol", "sub")), P(("groups", "uv")), P(), P(), P())
    out_specs = (P(("groups", "uv", "pol", "sub"), None, None), P(("groups", "uv", "pol", "sub")))
    return jax.shard_map(shards, mesh=mesh, in_specs=in_specs, out_specs=out_specs, check_vma=False)
```

profile of v0, /device:TPU:0, one launch (start us, length us, event | category | flops | bytes accessed | tf_op | source)
XLA Modules:
  0.0 795.8 jit_solution(5974640794278466336)
XLA Ops:
  7.2 0.0 copy-start
  7.2 0.0 reduce-scatter.2.cloned.1.call-start
  7.2 0.0 copy-start.1
  7.3 9.2 %fusion.27 = f32[128,128,128]{2,0,1:T(8,128)} fusion(bf16[2,128,128,128]{3,2,1,0:T(8,128)(2,1)} %param.5), kind=kOutput, calls=%fused_computation.30 | convolution fusion | flops 3221454848 | bytes 12582912 | tf_op jit(solution)/shard_map/ft,ctk->cfk/dot_general | solution.py:23
  16.4 0.0 copy-done.1
  16.5 0.0 copy-start.4
  16.5 6.0 fusion.25
  22.4 0.0 copy-done
  22.5 0.1 copy.26
  22.6 0.0 copy-done.4
  22.6 9.3 %add_multiply_fusion = f32[128,128,128]{2,0,1:T(8,128)S(1)} fusion(f32[128,128,128]{2,0,1:T(8,128)} %fusion.27, f32[128]{0:T(128)S(1)} %convert_element_type.36, bf16[2,128,128,128]{3,2,1,0:T(8,128)(2,1)} %param.5), kind=kOutput, calls=%fused_computation.27 | convolution fusion | flops 3225649152 | bytes 20972032 | tf_op jit(solution)/shard_map/ft,ctk->cfk/dot_general | solution.py:23
  32.0 9.3 %subtract_multiply_fusion = f32[128,128,128]{2,0,1:T(8,128)S(1)} fusion(f32[128,128,128]{2,0,1:T(8,128)} %fusion.25, f32[128]{0:T(128)S(1)} %convert_element_type.36, bf16[2,128,128,128]{3,2,1,0:T(8,128)(2,1)} %param.5), kind=kOutput, calls=%fused_computation.26 | convolution fusion | flops 3225649152 | bytes 20972032 | tf_op jit(solution)/shard_map/ft,ctk->cfk/dot_general | solution.py:26
  41.3 167.0 %fusion.81 = f32[512,128]{0,1:T(8,128)S(1)} fusion(f32[128,128,128]{2,0,1:T(8,128)S(1)} %add_multiply_fusion, s32[128]{0:T(128)S(1)} %compare_select_fusion, s32[512,128]{0,1:T(8,128)S(1)} %copy.26), kind=kOutput, calls=%fused_computation.56 | convolution fusion | flops 13002342400 | bytes 8913408 | tf_op jit(solution)/shard_map/dot_general | solution.py:65
  208.3 166.8 %fusion.86 = f32[512,128]{0,1:T(8,128)S(1)} fusion(f32[128,128,128]{2,0,1:T(8,128)S(1)} %subtract_multiply_fusion, s32[128]{0:T(128)S(1)} %compare_select_fusion, s32[512,128]{0,1:T(8,128)S(1)} %copy.26), kind=kOutput, calls=%fused_computation.57 | convolution fusion | flops 13002342400 | bytes 8913408 | tf_op jit(solution)/shard_map/dot_general | solution.py:68
  375.1 168.4 %fusion.61 = f32[512,128]{0,1:T(8,128)S(1)} fusion(f32[512,128]{0,1:T(8,128)S(1)} %fusion.81, f32[128,128,128]{2,0,1:T(8,128)S(1)} %subtract_multiply_fusion, s32[128]{0:T(128)S(1)} %compare_select_fusion, s32[512,128]{0,1:T(8,128)S(1)} %copy.26), kind=kOutput, calls=%fused_computation.52 | convolution fusion | flops 13002473472 | bytes 9175552 | tf_op jit(solution)/shard_map/dot_general | solution.py:65
  543.5 0.0 copy-start.2
  543.5 0.0 copy-start.3
  543.6 168.4 %fusion.76 = f32[512,128]{0,1:T(8,128)S(1)} fusion(f32[512,128]{0,1:T(8,128)S(1)} %fusion.86, f32[128,128,128]{2,0,1:T(8,128)S(1)} %add_multiply_fusion, s32[128]{0:T(128)S(1)} %compare_select_fusion, s32[512,128]{0,1:T(8,128)S(1)} %copy.26), kind=kOutput, calls=%fused_computation.55 | convolution fusion | flops 13002473472 | bytes 9175552 | tf_op jit(solution)/shard_map/dot_general | solution.py:68
  712.0 0.8 pad_maximum_fusion
  712.8 0.0 reduce-scatter.2.cloned.1.call-update
  712.8 24.7 %reduce-scatter.2.cloned.1.call-done = f32[128,256]{0,1:T(8,128)} async-done(((f32[512,256]{0,1:T(8,128)}), f32[128,256]{0,1:T(8,128)}) %reduce-scatter.2.cloned.1.call-update) | async-done | bytes 131088 | tf_op jit(solution)/shard_map/reduce_scatter | solution.py:92
  737.6 1.7 copy.31
  739.2 3.6 all-to-all-start
  742.8 0.0 copy-done.2
  742.8 1.0 fusion.110
  743.9 3.3 all-to-all-done
  747.2 0.0 copy-done.3
  747.2 8.2 %fusion.17 = f32[32,128,128]{2,1,0:T(8,128)S(1)} fusion(f32[128,512]{1,0:T(8,128)S(1)} %get-tuple-element.7, f32[32,512]{1,0:T(8,128)S(1)} %get-tuple-element.5, f32[128,512]{1,0:T(8,128)S(1)} %get-tuple-element.6, f32[32,512]{1,0:T(8,128)S(1)} %get-tuple-element.4, s32[512]{0:T(512)S(1)} %copy-done.3), kind=kOutput, calls=%fused_computation.18 | convolution fusion | flops 3228434432 | bytes 2754560 | tf_op jit(solution)/shard_map/dlk,km->dlm/dot_general | solution.py:56
  755.3 33.1 %multiply_reduce_fusion = (f32[32]{0:T(128)S(1)}, f32[32]{0:T(128)S(1)}, f32[32,128,128]{2,1,0:T(8,128)}) fusion(f32[32,128,128]{2,1,0:T(8,128)S(1)} %fusion.17, s32[512]{0:T(512)S(1)} %copy-done.3, f32[128,512]{1,0:T(8,128)S(1)} %get-tuple-element.7, f32[32,512]{1,0:T(8,128)S(1)} %get-tuple-element.5, f32[128,512]{1,0:T(8,128)S(1)} %get-tuple-element.6, ...), kind=kOutput, calls=%fused_computation.48 | convolution fusion | flops 3231055872 | bytes 4851968 | tf_op jit(solution)/shard_map/dlk,km->dlm/dot_general | solution.py:56
  788.5 0.5 rsqrt_multiply_fusion
  (6 shorter events, 0.1 us)
Async XLA Ops:
  7.2 15.3 %copy-start = (s32[512,512]{1,0:T(8,128)S(1)}, s32[512,512]{1,0:T(8,128)}, u32[]{:S(2)}) copy-start(s32[512,512]{1,0:T(8,128)} %param.7) | copy-start | bytes 3145732
  7.2 730.4 %reduce-scatter.2.cloned.1.call-start = ((), (), s32[]{:S(2)}) async-start(), calls=%async_computation.2 | async-start | bytes 655360 | tf_op jit(solution)/shard_map/reduce_scatter | solution.py:92
  7.2 9.2 %copy-start.1 = (bf16[2,128,128,128]{3,2,1,0:T(8,128)(2,1)S(1)}, bf16[2,128,128,128]{3,2,1,0:T(8,128)(2,1)}, u32[]{:S(2)}) copy-start(bf16[2,128,128,128]{3,2,1,0:T(8,128)(2,1)} %param.5) | copy-start | bytes 25165828
  16.5 6.2 copy-start.4
  543.5 199.3 %copy-start.2 = (s32[512]{0:T(512)S(1)}, s32[512]{0:T(512)}, u32[]{:S(2)}) copy-start(s32[512]{0:T(512)} %param.8) | copy-start | bytes 6148
  543.5 203.6 %copy-start.3 = (s32[512]{0:T(512)S(1)}, s32[512]{0:T(512)}, u32[]{:S(2)}) copy-start(s32[512]{0:T(512)} %param.9) | copy-start | bytes 6148
  739.2 7.9 all-to-all-start
Sparse Core Ops, SparseCore 0:
  712.9 24.5 reduce-scatter.1
where the time goes:
time: 796 us
  matrix products  746 us (94%)
  waiting for transfers between devices  28 us (4%)
  between operations  14.2 us (2%)
    dot_general x1, matrix products, dedisperse(): jnp.dot(sine, right_imag, precision=precise)  168 us
    dot_general x1, matrix products, dedisperse(): jnp.dot(sine, right_real, precision=precise)  168 us
    dot_general x1, matrix products, dedisperse(): jnp.dot(cosine, right_real, precision=precise)  167 us
    dot_general x1, matrix products, dedisperse(): jnp.dot(cosine, right_imag, precision=precise)  167 us
    dot_general x1, matrix products, picture(): jnp.einsum('dlk,km->dlm', first, jnp.cos(column_angle), precision=precise)  33.1 us
    reduce_scatter x1, waiting for transfers between devices, shards(): lax.psum_scatter(jnp.concatenate([part_real, part_imag], axis=1), 'uv', s...  24.7 us
  transfers between devices with their start and end apart: 2, of which 2 were waited for; matrix products, arithmetic and copies ran while one was open for 0% of the time, Pallas kernels for 0%

commit v1 on v0

v1 whole, which is shorter than its diff:
```python
import functools
import math

import jax
import jax.numpy as jnp
import numpy as np
from jax import lax
from jax.experimental import pallas as pl
from jax.experimental.pallas import tpu as pltpu
from jax.sharding import PartitionSpec as P

IMG = 128
FRAC = 8
AXES = ("uv", "pol", "sub")
F32 = jnp.float32
BF16 = jnp.bfloat16


def time_tables(times):
    t = np.arange(times)
    cot = np.where(t == 0, 2.0**60, 1.0 / np.tan(np.pi * np.where(t == 0, 1, t) / times))
    cot[times // 2] = 0.0
    cot = cot.astype(np.float32).astype(np.float64)
    power = 2.0 ** np.floor(16 - np.log2(np.maximum(np.abs(cot), 2.0**-10)))
    shifted = cot * power - np.where(t % 2 == 0, 1.0, -1.0) / times
    folded = np.minimum(t, times // 2)
    rows = [np.sin(np.pi * folded / times), np.cos(np.pi * folded / times), power, shifted]
    table = np.repeat(np.stack(rows), 8, axis=0).astype(np.float32)
    column = np.repeat(cot[:, None], 128, axis=1).astype(np.float32)
    return table, column


def coefficients(n, table, times):
    cycle = FRAC * times
    lanes = table.shape[1]
    parts = [[], [], [], []]
    for j in range(n.shape[1] // lanes):
        part = n[:, j * lanes : (j + 1) * lanes]
        fold = jnp.minimum(part, cycle - part)
        for i in range(4):
            index = (fold if i < 2 else part) >> 3
            parts[i].append(jnp.take_along_axis(table[i * 8 : (i + 1) * 8], index, axis=1))
    sin_q, cos_q, power, shifted = [jnp.concatenate(p, axis=1) for p in parts]
    fold = jnp.minimum(n, cycle - n)
    theta = (fold & (FRAC - 1)).astype(F32) * (math.pi / cycle)
    square = theta * theta
    cos_r = 1.0 - square * (0.5 - square * (1.0 / 24.0))
    sin_r = theta * (1.0 - square * (1.0 / 6.0 - square * (1.0 / 120.0)))
    sin_a = sin_q * cos_r + cos_q * sin_r
    cos_a = cos_q * cos_r - sin_q * sin_r
    cos_a = jnp.where(n + n > cycle, -cos_a, cos_a)
    r = n & (FRAC - 1)
    side = jnp.abs(r - FRAC // 2)
    size = [math.cos(math.pi * i / FRAC) for i in range(FRAC // 2)]
    s = jnp.where(side == 0, size[0], jnp.where(side == 1, size[1], jnp.where(side == 2, size[2], size[3])))
    s = jnp.where((n & FRAC) == 0, s, -s)
    whole = r == 0
    ratio = sin_a / s
    u = jnp.where(whole, power, sin_a * ratio)
    w = jnp.where(whole, shifted, cos_a * ratio)
    k = jnp.where(whole, 0.0, s * cos_a / jnp.where(whole, 1.0, sin_a))
    return u, w, k, jnp.where(whole, 0.0, s)


def dedisperse_kernel(
    flags_ref, delays_ref, table_ref, column_ref, sign_ref, vis_hbm, out_ref,
    vis_ref, sem, acc_ref, u_ref, w_ref, k_ref, sums_ref, *pairs,
    channels, times, cells, block, group, copies, scale,
):
    trials = delays_ref.shape[2]
    per = channels // copies

    def copy(i, p):
        rows = pl.ds(i * per, per)
        return pltpu.make_async_copy(vis_hbm.at[p, rows], vis_ref.at[p, rows], sem.at[p, i])

    for i in range(copies):
        for p in range(2):
            copy(i, p).start()
    table = table_ref[...]

    def prepare(i, carry):
        u, w, k, s = coefficients(delays_ref[i], table, times)
        u_ref[i] = u
        w_ref[i] = w
        rows = pl.ds(pl.multiple_of(i * 8, 8), 8)
        k_ref[rows, :] = k
        k_ref[pl.ds(pl.multiple_of(channels + i * 8, 8), 8), :] = s
        return carry

    lax.fori_loop(0, channels // 8, prepare, 0)
    acc_ref[...] = jnp.zeros_like(acc_ref)
    sign_rows = sign_ref[...]
    column_sign = jnp.where(lax.broadcasted_iota(jnp.int32, (8, cells), 0) % 2 == 0, 1.0, -1.0)

    def body(step, carry):
        total = None
        for i in range(block // group):
            right, left = pairs[2 * i], pairs[2 * i + 1]
            for j in range(group):
                at = i * group + j
                c = step * block + at
                keep = flags_ref[c].astype(F32)
                signs = (sign_rows * keep).astype(BF16)
                for p in range(2):
                    sample = vis_ref[p, c]
                    left[p * cells : (p + 1) * cells, j * times : (j + 1) * times] = sample.T * signs
                    wide = sample.astype(F32)
                    part = wide[0:8]
                    for t in range(8, times, 8):
                        part = part + wide[t : t + 8]
                    row = jnp.sum(part * column_sign, axis=0, keepdims=True) * keep
                    sums_ref[step * (block // 8) + at // 8, at % 8 : at % 8 + 1, p * cells : (p + 1) * cells] = row
                for b in range(0, trials, 128):
                    row = step * (block // 8) + at // 8
                    u = u_ref[row, at % 8 : at % 8 + 1, b : b + 128]
                    w = w_ref[row, at % 8 : at % 8 + 1, b : b + 128]
                    for t in range(0, times, 16):
                        bottom = column_ref[t : t + 16, :] * u - w
                        guess = pltpu.reciprocal(bottom, approx=True)
                        high = guess.astype(BF16)
                        rest = (1.0 - bottom * high.astype(F32)) * guess
                        rows = slice(j * times + t, j * times + t + 16)
                        right[rows, b : b + 128] = high
                        right[rows, trials + b : trials + b + 128] = rest.astype(BF16)
            one = jnp.dot(left[...], right[...], preferred_element_type=F32)
            total = one if total is None else total + one
        acc_ref[...] += total
        return carry

    steps = channels // block // copies
    for i in range(copies):
        for p in range(2):
            copy(i, p).wait()
        lax.fori_loop(i * steps, (i + 1) * steps, body, 0)

    sums = sums_ref[...].reshape(channels, 2 * cells)
    real, imag = sums[:, :cells], sums[:, cells:]
    lower = jnp.concatenate([imag, -real], axis=1)
    right = jnp.concatenate([sums, lower], axis=0)
    extra = jnp.dot(k_ref[...].T, right, precision=lax.Precision.HIGHEST, preferred_element_type=F32)
    main = (acc_ref[:, :trials] + acc_ref[:, trials:]).T
    out_ref[...] = (main + extra) * scale


def dedisperse(flags, delays, visibilities, scale):
    _, channels, times, cells = visibilities.shape
    trials = delays.shape[2]
    table, column = time_tables(times)
    sign = np.where(np.arange(times) % 2 == 0, 1.0, -1.0).astype(np.float32)[None, :]
    block = min(16, channels)
    group = 2
    copies = min(4, channels // block)
    vmem = pl.BlockSpec(memory_space=pltpu.VMEM)
    scratch = [
        pltpu.VMEM(visibilities.shape, visibilities.dtype),
        pltpu.SemaphoreType.DMA((2, copies)),
        pltpu.VMEM((2 * cells, 2 * trials), F32),
        pltpu.VMEM((channels // 8, 8, trials), F32),
        pltpu.VMEM((channels // 8, 8, trials), F32),
        pltpu.VMEM((2 * channels, trials), F32),
        pltpu.VMEM((channels // 8, 8, 2 * cells), F32),
    ]
    for _ in range(block // group):
        scratch += [pltpu.VMEM((group * times, 2 * trials), BF16), pltpu.VMEM((2 * cells, group * times), BF16)]
    return pl.pallas_call(
        functools.partial(
            dedisperse_kernel, channels=channels, times=times, cells=cells,
            block=block, group=group, copies=copies, scale=scale,
        ),
        in_specs=[pl.BlockSpec(memory_space=pltpu.SMEM), vmem, vmem, vmem, vmem, pl.BlockSpec(memory_space=pl.ANY)],
        out_specs=vmem,
        out_shape=jax.ShapeDtypeStruct((trials, 2 * cells), F32),
        scratch_shapes=scratch,
        compiler_params=pltpu.CompilerParams(vmem_limit_bytes=60 << 20),
        name="dedisperse",
    )(flags, delays, jnp.asarray(table), jnp.asarray(column), jnp.asarray(sign), visibilities)


def image_kernel(sums_ref, cos_ref, sin_ref, right_ref, image_ref, snr_ref, real_ref, imag_ref, peak_ref, power_ref, *, side, weight):
    blocks = sums_ref.shape[1]
    trials = sums_ref.shape[2]
    cells = sums_ref.shape[3] // 2
    for b in range(blocks):
        total = sums_ref[0, b]
        for i in range(1, sums_ref.shape[0]):
            total = total + sums_ref[i, b]
        total = total * weight
        real_ref[:, b * cells : (b + 1) * cells] = total[:, :cells]
        imag_ref[:, b * cells : (b + 1) * cells] = total[:, cells:]
    right = right_ref[...]
    for d in range(trials):
        real = real_ref[d : d + 1, :]
        imag = imag_ref[d : d + 1, :]
        cosine, sine = cos_ref[...], sin_ref[...]
        first = real * cosine - imag * sine
        second = -(real * sine + imag * cosine)
        left = jnp.concatenate([first, second], axis=1)
        high = left.astype(BF16)
        low = (left - high.astype(F32)).astype(BF16)
        one = jnp.dot(jnp.concatenate([high, low], axis=0), right, preferred_element_type=F32)
        image = one[:side, :side] + (one[:side, side:] + one[side:, :side])
        image_ref[d] = image
        peak_ref[d : d + 1, :] = jnp.max(image, axis=0, keepdims=True)
        power_ref[d : d + 1, :] = jnp.sum(image * image, axis=0, keepdims=True)
    peak = jnp.max(peak_ref[...], axis=1, keepdims=True)
    power = jnp.sum(power_ref[...], axis=1, keepdims=True) / (side * side)
    snr_ref[...] = peak / jnp.sqrt(power + 1e-06)


def picture(sums, coord_u, coord_v, side, weight):
    total = coord_u.shape[0]
    trials = sums.shape[2]
    pixels = jnp.arange(side, dtype=jnp.int32)
    row_angle = (pixels[:, None] * coord_u[None, :] % side).astype(F32) * (2.0 * math.pi / side)
    column_angle = (coord_v[:, None] * pixels[None, :] % side).astype(F32) * (2.0 * math.pi / side)
    columns = jnp.concatenate([jnp.cos(column_angle), jnp.sin(column_angle)], axis=0)
    high = lax.reduce_precision(columns, 8, 7)
    right = jnp.concatenate([high.astype(BF16), (columns - high).astype(BF16)], axis=1)
    vmem = pl.BlockSpec(memory_space=pltpu.VMEM)
    images, snr = pl.pallas_call(
        functools.partial(image_kernel, side=side, weight=weight),
        in_specs=[vmem] * 4,
        out_specs=[vmem] * 2,
        out_shape=[jax.ShapeDtypeStruct((trials, side, side), F32), jax.ShapeDtypeStruct((trials, 1), F32)],
        scratch_shapes=[pltpu.VMEM((trials, total), F32)] * 2 + [pltpu.VMEM((trials, side), F32)] * 2,
        compiler_params=pltpu.CompilerParams(vmem_limit_bytes=60 << 20),
        name="picture",
    )(sums, jnp.cos(row_angle), jnp.sin(row_angle), right)
    return images, snr[:, 0]


def shards(visibilities, flags, delays, coord_u, coord_v, *, sizes):
    channels = visibilities.shape[1]
    times = visibilities.shape[2]
    cells = visibilities.shape[3]
    trials, total_channels = delays.shape
    position = lax.axis_index("uv")
    rows = lax.dynamic_slice_in_dim(delays, position * channels, channels, 1).T
    scale = 1.0 / math.sqrt(total_channels * times)
    part = dedisperse(flags, rows.reshape(channels // 8, 8, trials), visibilities, scale)
    owners = sizes["uv"] * sizes["pol"] * sizes["sub"]
    held = lax.all_to_all(part.reshape(owners, trials // owners, 2 * cells), AXES, split_axis=0, concat_axis=0, tiled=True)
    held = held.reshape(sizes["uv"], sizes["pol"] * sizes["sub"], trials // owners, 2 * cells)
    weight = 2.0 / math.sqrt(coord_u.shape[0])
    return picture(held, coord_u, coord_v, IMG, weight)


def solution(mesh):
    in_specs = (P(None, "uv", "groups", ("pol", "sub")), P(("groups", "uv")), P(), P(), P())
    out_specs = (P(("groups", "uv", "pol", "sub"), None, None), P(("groups", "uv", "pol", "sub")))
    body = functools.partial(shards, sizes=dict(mesh.shape))
    return jax.shard_map(body, mesh=mesh, in_specs=in_specs, out_specs=out_specs, check_vma=False)
```

time: 796 us -> 61 us (0.08)
  matrix products: 746 us -> 0 us
  Pallas kernels: 0 us -> 34.1 us
  waiting for transfers between devices: 28 us -> 10.4 us
  between operations: 14.2 us -> 0.71 us
    dot_general x10 -> x0, matrix products: 746 us -> none  [the longest x1 168 us: dedisperse(): jnp.dot(sine, right_imag, precision=precise)]
    pallas_call x0 -> x2, Pallas kernels: none -> 34.1 us  [the longest x1 26.4 us: dedisperse(): pl.pallas_call(functools.partial(dedisperse_kernel, channels=channels, ti...]
    reduce_scatter x1 -> x0, waiting for transfers between devices: 24.7 us -> none  [shards(): lax.psum_scatter(jnp.concatenate([part_real, part_imag], axis=1), 'uv', s...]
  transfers between devices with their start and end apart: 2 -> 1, of which waited for: 2 -> 1; matrix products, arithmetic and copies ran while one was open for 0% -> 6% of each run, Pallas kernels for 0% -> 0%
where the time goes in v1:
time: 61 us; the launch traced here: 60.7 us
  Pallas kernels  34.1 us (56%)
  waiting for transfers between devices  10.4 us (17%)
  starting transfers between devices  7.41 us (12%)
  other arithmetic  5.18 us (8%)
  local copies, waits for them, and re-layouts  2.86 us (5%)
  between operations  0.71 us (1%)
    pallas_call x1, Pallas kernels, dedisperse(): pl.pallas_call(functools.partial(dedisperse_kernel, channels=channels, ti...  26.4 us
    all_to_all x1, waiting for transfers between devices, shards(): lax.all_to_all(part.reshape(owners, trials // owners, 2 * cells), AXES, s...  10.4 us
    pallas_call x1, Pallas kernels, picture(): pl.pallas_call(functools.partial(image_kernel, side=side, weight=weight),...  7.71 us
    all_to_all x1, starting transfers between devices, shards(): lax.all_to_all(part.reshape(owners, trials // owners, 2 * cells), AXES, s...  7.41 us
    unnamed x8, local copies, waits for them, and re-layouts  2 us
    sin x1, other arithmetic, picture(): jnp.sin(row_angle)  1.81 us
    pallas_call x1, other arithmetic, picture(): pl.pallas_call(functools.partial(image_kernel, side=side, weight=weight),...  1.34 us
  transfers between devices with their start and end apart: 1, of which 1 were waited for; matrix products, arithmetic and copies ran while one was open for 6% of the time, Pallas kernels for 0%

profile of v1, /device:TPU:0, one launch (start us, length us, event | category | flops | bytes accessed | tf_op | source)
XLA Modules:
  0.0 60.7 jit_solution(7382131784140673035)
XLA Ops:
  0.6 0.0 copy-start
  0.6 0.0 copy-start.2
  0.7 0.0 copy-start.3
  0.7 1.2 %copy-done = s32[512,512]{1,0:T(8,128)S(1)} copy-done((s32[512,512]{1,0:T(8,128)S(1)}, s32[512,512]{1,0:T(8,128)}, u32[]{:S(2)}) %copy-start) | copy-done | bytes 1048600
  1.9 0.8 %copy.11 = s32[128,512]{1,0:T(8,128)} copy(s32[128,512]{0,1:T(8,128)S(1)} %dynamic-slice_bitcast_fusion) | data formatting | bytes 524288 | tf_op jit(solution)/shard_map/transpose | solution.py:239
  2.7 26.4 %dedisperse.1 = f32[512,256]{1,0:T(8,128)} custom-call(s32[128]{0:T(128)} %flags_ref.1, s32[16,8,512]{2,1,0:T(8,128)} %bitcast.7, f32[32,128]{1,0:T(8,128)} %constant.40.clone.table_ref, f32[128,128]{1,0:T(8,128)} %constant.41.clone.column_ref, f32[1,128]{1,0:T(1,128)} %constant.42.clone.sign_ref, bf16[2,128,128,128]{3,2,1,0:T(8,128)(2,1)} %vis_hbm.1), custom_call_target="tpu_custom_call" | custom-call | tf_op jit(solution)/shard_map/dedisperse/pallas_call | solution.py:166
  29.1 7.4 %all-to-all-start = ((f32[16,32,256]{2,1,0:T(8,128)}), f32[16,32,256]{2,1,0:T(8,128)S(1)}, u32[]{:S(2)}, u32[]{:S(2)}) async-start(f32[16,32,256]{2,1,0:T(8,128)} %bitcast.6), calls=%async_computation | async-start | bytes 1048576 | tf_op jit(solution)/shard_map/all_to_all | solution.py:243
  36.6 0.0 copy-done.2
  36.6 1.1 %fusion.14 = (f32[512,128]{1,0:T(8,128)S(1)}, f32[512,128]{1,0:T(8,128)S(1)}) fusion(s32[512]{0:T(512)S(1)} %copy-done.2), kind=kLoop, calls=%fused_computation.25 | loop fusion | flops 917504 | bytes 526336 | tf_op jit(solution)/shard_map/cos | solution.py:217
  37.7 0.1 reduce-precision_convert_fusion
  37.8 0.8 %pad_maximum_fusion.1.right_ref = bf16[1024,256]{1,0:T(8,128)(2,1)} fusion(bf16[1024,128]{1,0:T(8,128)(2,1)S(1)} %get-tuple-element.7, bf16[1024,128]{1,0:T(8,128)(2,1)S(1)} %get-tuple-element.6), kind=kLoop, calls=%fused_computation.4 | loop fusion | flops 1048576 | bytes 1048576 | tf_op jit(solution)/shard_map/concatenate | solution.py:219
  38.6 0.0 copy-done.3
  38.6 1.8 %fusion.15 = (f32[128,512]{1,0:T(8,128)}, f32[128,512]{1,0:T(8,128)}) fusion(s32[512]{0:T(512)S(1)} %copy-done.3), kind=kLoop, calls=%fused_computation.26 | loop fusion | flops 917504 | bytes 526336 | tf_op jit(solution)/shard_map/sin | solution.py:229
  40.4 10.4 %all-to-all-done = f32[16,32,256]{2,1,0:T(8,128)S(1)} async-done(((f32[16,32,256]{2,1,0:T(8,128)}), f32[16,32,256]{2,1,0:T(8,128)S(1)}, u32[]{:S(2)}, u32[]{:S(2)}) %all-to-all-start) | async-done | bytes 524320 | tf_op jit(solution)/shard_map/all_to_all | solution.py:243
  50.8 0.0 copy-start.1
  50.8 0.8 %copy-done.1 = f32[16,32,256]{2,1,0:T(8,128)} copy-done((f32[16,32,256]{2,1,0:T(8,128)}, f32[16,32,256]{2,1,0:T(8,128)S(1)}, u32[]{:S(2)}) %copy-start.1) | copy-done | bytes 524312
  51.6 7.7 %picture.1 = (f32[32,128,128]{2,1,0:T(8,128)}, f32[32,1]{1,0:T(8,128)}) custom-call(f32[4,4,32,256]{3,2,1,0:T(8,128)} %bitcast.5, f32[128,512]{1,0:T(8,128)} %get-tuple-element.11.cos_ref, f32[128,512]{1,0:T(8,128)} %get-tuple-element.10.sin_ref, bf16[1024,256]{1,0:T(8,128)(2,1)} %pad_maximum_fusion.1.right_ref), custom_call_target="tpu_custom_call" | custom-call | tf_op jit(solution)/shard_map/picture/pallas_call | solution.py:221
  59.3 1.3 %reduce = f32[32]{0:T(128)} reduce(f32[32,1]{1,0:T(8,128)} %get-tuple-element.5, f32[]{:T(128)} %constant.43), dimensions={1}, to_apply=%get-tuple-element.5.reduce_sub_computation | reduce | bytes 260 | tf_op jit(solution)/shard_map/picture/pallas_call | solution.py:221
  (1 shorter events, 0.0 us)
Async XLA Ops:
  0.6 1.2 %copy-start = (s32[512,512]{1,0:T(8,128)S(1)}, s32[512,512]{1,0:T(8,128)}, u32[]{:S(2)}) copy-start(s32[512,512]{1,0:T(8,128)} %param.10) | copy-start | bytes 3145732
  0.6 35.9 %copy-start.2 = (s32[512]{0:T(512)S(1)}, s32[512]{0:T(512)}, u32[]{:S(2)}) copy-start(s32[512]{0:T(512)} %param.12) | copy-start | bytes 6148
  0.7 38.0 %copy-start.3 = (s32[512]{0:T(512)S(1)}, s32[512]{0:T(512)}, u32[]{:S(2)}) copy-start(s32[512]{0:T(512)} %param.11) | copy-start | bytes 6148
  29.1 21.7 %all-to-all-start = ((f32[16,32,256]{2,1,0:T(8,128)}), f32[16,32,256]{2,1,0:T(8,128)S(1)}, u32[]{:S(2)}, u32[]{:S(2)}) async-start(f32[16,32,256]{2,1,0:T(8,128)} %bitcast.6), calls=%async_computation | async-start | bytes 1048576 | tf_op jit(solution)/shard_map/all_to_all | solution.py:243
  50.8 0.8 %copy-start.1 = (f32[16,32,256]{2,1,0:T(8,128)}, f32[16,32,256]{2,1,0:T(8,128)S(1)}, u32[]{:S(2)}) copy-start(f32[16,32,256]{2,1,0:T(8,128)S(1)} %all-to-all-done) | copy-start | bytes 1572868
